TPU v7x, 32 devices: a whole 2x2x4 slice. The times are simulated.
32 devices in a mesh: parts: 2 (over x), tm: 8 (over z, y), stn: 2 (over core).
Axes of the slice: x: 2, y: 2, z: 4, core: 2. Of those that a mesh axis runs over, the one named last changes fastest.
Arguments:
- voltages: bfloat16 [256, 2, 32, 2, 2048], P(('parts', 'stn'), None, 'tm'), parts along dimension 0, may hold values from -6 to 6
- filter_taps: float32 [16, 2048], replicated, may hold values from -1.5 to 1.5
- use_mask: int32 [512, 8], P('parts'), parts along dimension 0, may hold values 0 or 1
- block_index: int32 [512, 8], P('parts'), parts along dimension 0, may hold values from 0 to 127
- weight_blocks: bfloat16 [128, 512], P('tm'), may hold values from -0.5 to 0.5
Outputs:
- power: float32 [2048, 32, 512], P('stn', 'tm', 'parts'), parts along dimension 2
There are 2 independent parts, one for each index of `parts`. A program takes and returns all parts, laid end to end along the dimension named above; an argument that names none is the same for every part. Nothing has to cross between parts.
All inputs are finite; a program needn't handle non-finite values.
Results may differ from a plain program's by a relative error of at most 0.008.
Values may be sent and summed in bfloat16 or wider, within the bound.
A program may use at most 192 MiB of HBM per device.

v0:
```python
import math

import jax
import jax.numpy as jnp
from jax import lax
from jax.sharding import PartitionSpec as P

P_SIZE = 64
SB = 16
G = 16


def from_behind(block, axis, distance):
    devices = range(lax.axis_size(axis))
    route = [(i - distance, i) for i in devices if i - distance in devices]
    return lax.ppermute(block, axis, route)


def transform_tables(first_size, second_size):
    full_size = first_size * second_size
    first_range = jnp.arange(first_size, dtype=jnp.int32)
    second_range = jnp.arange(second_size, dtype=jnp.int32)
    first_angle = (first_range[:, None] * first_range[None, :] % first_size).astype(jnp.float32) * (
        2.0 * math.pi / first_size
    )
    cosine_first = jnp.cos(first_angle)
    sine_first = jnp.sin(first_angle)
    section_one = jnp.stack(
        [
            jnp.stack([cosine_first, -sine_first], axis=1),
            jnp.stack([sine_first, cosine_first], axis=1),
        ],
        axis=0,
    )
    second_angle = (second_range[:, None] * second_range[None, :] % second_size).astype(
        jnp.float32
    ) * (2.0 * math.pi / second_size)
    cosine_second = jnp.cos(second_angle)
    sine_second = jnp.sin(second_angle)
    section_two = jnp.stack(
        [
            jnp.stack([cosine_second, sine_second], axis=-1),
            jnp.stack([-sine_second, cosine_second], axis=-1),
        ],
        axis=1,
    )
    section_two = section_two.reshape(2 * second_size, 2 * second_size)
    twist_angle = (second_range[:, None] * first_range[None, :] % full_size).astype(jnp.float32) * (
        2.0 * math.pi / full_size
    )
    return (
        section_one.astype(jnp.bfloat16),
        jnp.cos(twist_angle),
        jnp.sin(twist_angle),
        section_two.astype(jnp.bfloat16),
    )


def filter_frames(window, filter_taps, frame_count):
    history = filter_taps.shape[0] - 1
    shape_out = window.shape[:2] + (frame_count,) + window.shape[3:]
    summed = jnp.zeros(shape_out, jnp.float32)
    for tap_index in range(filter_taps.shape[0]):
        sliced = lax.slice_in_dim(
            window, history - tap_index, history - tap_index + frame_count, axis=2
        )
        summed = summed + filter_taps[tap_index] * sliced.astype(jnp.float32)
    return summed.astype(jnp.bfloat16)


def channelize(filtered, tables):
    section_one, twist_cos, twist_sin, section_two = tables
    first_size = section_one.shape[1]
    second_size = twist_cos.shape[0]
    station_count, frame_count = (filtered.shape[0], filtered.shape[2])
    reshaped = filtered.reshape(station_count, 2, frame_count, 2, first_size, second_size)
    first_section = jnp.einsum(
        "spfrae,raob->spfeob", reshaped, section_one, preferred_element_type=jnp.float32
    )
    real_part = first_section[:, :, :, :, 0, :]
    imag_part = first_section[:, :, :, :, 1, :]
    norm_factor = 1.0 / math.sqrt(first_size * second_size)
    twist_real = (real_part * twist_cos + imag_part * twist_sin) * norm_factor
    twist_imag = (imag_part * twist_cos - real_part * twist_sin) * norm_factor
    twiddled = jnp.stack([twist_real, twist_imag], axis=-2).astype(jnp.bfloat16)
    twiddled = twiddled.reshape(station_count, 2, frame_count, 2 * second_size, first_size)
    spectra = jnp.einsum(
        "dk,spfkb->spfdb", section_two, twiddled, preferred_element_type=jnp.float32
    )
    return spectra.astype(jnp.bfloat16).reshape(
        station_count, 2, frame_count, second_size, 2, first_size
    )


def beam_matrix(use_rows, picked):
    beam_count, block_count = use_rows.shape
    shaped = (
        picked.reshape(beam_count, block_count, G, 2, SB)
        * use_rows.astype(jnp.bfloat16)[:, :, None, None, None]
    )
    real_part = shaped[:, :, :, 0, :].transpose(2, 1, 3, 0).reshape(G, block_count * SB, beam_count)
    imag_part = shaped[:, :, :, 1, :].transpose(2, 1, 3, 0).reshape(G, block_count * SB, beam_count)
    upper_rows = jnp.stack([real_part, imag_part], axis=2)
    lower_rows = jnp.stack([-imag_part, real_part], axis=2)
    return jnp.stack([upper_rows, lower_rows], axis=1)


def form_beams(row_block, weights):
    row_count = row_block.shape[0]
    group_count = weights.shape[0]
    reshaped = row_block.reshape(group_count, -1, row_block.shape[2])
    matrices = weights.reshape(group_count, row_block.shape[2], -1)
    product = jnp.einsum("gmk,gkn->gmn", reshaped, matrices, preferred_element_type=jnp.float32)
    return product.reshape(row_count, -1)


def detect(summed):
    shaped = summed.reshape(summed.shape[0], 4, -1)
    return jnp.sum(shaped * shaped, axis=1)


def body(voltages, filter_taps, use_mask, block_index, weight_blocks):
    stations = voltages.shape[0]
    frames = voltages.shape[2]
    channels = voltages.shape[4]
    history = filter_taps.shape[0] - 1
    reaches = -(-history // frames)
    earlier = []
    for distance in range(reaches, 0, -1):
        lowest = max(0, distance * frames - history)
        earlier.append(from_behind(voltages[:, :, lowest:], "tm", distance))
    window = jnp.concatenate(earlier + [voltages], axis=2)
    filtered = filter_frames(window, filter_taps, frames)
    spectra = channelize(filtered, transform_tables(P_SIZE, channels // P_SIZE))
    turned = spectra.transpose(2, 3, 5, 1, 4, 0).reshape(frames, channels, 2, 2 * stations)
    blocks_local = stations // SB
    row_width = weight_blocks.shape[1]
    block_start = lax.axis_index("stn") * blocks_local
    use_rows = lax.dynamic_slice_in_dim(use_mask, block_start, blocks_local, 1)
    index_rows = lax.dynamic_slice_in_dim(block_index, block_start, blocks_local, 1)
    flat_index = index_rows.reshape(-1)
    shard_rows = lax.all_gather(weight_blocks, "tm", axis=0, tiled=True)
    block_ids = jnp.arange(shard_rows.shape[0], dtype=jnp.int32)
    onehot = (flat_index[:, None] == block_ids[None, :]).astype(jnp.bfloat16)
    picked = jnp.dot(onehot, shard_rows, preferred_element_type=jnp.float32)
    picked = picked.astype(jnp.bfloat16).reshape(
        index_rows.shape[0], index_rows.shape[1], row_width
    )
    matrix = beam_matrix(use_rows, picked)

    def frame_power(running, frame_rows):
        partial_value = form_beams(frame_rows, matrix)
        summed = lax.psum_scatter(
            partial_value.astype(jnp.bfloat16).astype(jnp.float32).astype(jnp.bfloat16),
            "stn",
            scatter_dimension=0,
            tiled=True,
        ).astype(jnp.float32)
        return (running, detect(summed))

    unused, detected = lax.scan(frame_power, jnp.zeros((), jnp.float32), turned)
    return detected.transpose(1, 0, 2)


def solution(mesh):
    in_specs = (
        P(("parts", "stn"), None, "tm", None, None),
        P(),
        P("parts", None),
        P("parts", None),
        P("tm", None),
    )
    out_specs = P("stn", "tm", "parts")
    return jax.shard_map(body, mesh=mesh, in_specs=in_specs, out_specs=out_specs, check_vma=False)
```

profile of v0, /device:TPU:13, one launch (start us, length us, event | category | flops | bytes accessed | tf_op | source)
XLA Modules:
  0.0 1031.0 jit_solution(15683490791320955258)
XLA Ops:
  6.5 6.5 copy.87
  13.0 4.3 collective-permute-start.2
  31.2 494.3 %all_gather.3 = bf16[128,512]{1,0:T(8,128)(2,1)S(1)} all-gather(bf16[16,512]{1,0:T(8,128)(2,1)S(1)} %copy-done.5), channel_id=1, replica_groups=mesh['parts'=2,'tm'=8,'stn'=2] {'tm'}, dimensions={0}, use_global_device_ids=true | all-gather | bytes 147456 | tf_op jit(solution)/shard_map/all_gather | solution.py:142
  526.0 8.2 reshape_reshape.3
  534.3 9.8 broadcast_multiply_fusion
  544.2 21.0 %fusion.38 = (bf16[256,4,16,1,16]{4,3,2,1,0:T(2,128)(2,1)}, bf16[256,4,16,1,16]{4,3,2,1,0:T(2,128)(2,1)}) fusion(bf16[256,4,16,2,16]{4,3,2,1,0:T(2,128)(2,1)S(1)} %broadcast_multiply_fusion), kind=kLoop, calls=%fused_computation.78 | loop fusion | bytes 2097152 | tf_op jit(solution)/shard_map/slice | solution.py:102
  565.2 17.6 %copy.117 = bf16[256,4,16,1,16]{0,4,1,2,3:T(8,128)(2,1)S(1)} copy(bf16[256,4,16,1,16]{4,3,2,1,0:T(2,128)(2,1)} %get-tuple-element.54) | data formatting | bytes 1048576 | tf_op jit(solution)/shard_map/transpose | solution.py:102
  582.8 17.6 %copy.116 = bf16[256,4,16,1,16]{0,4,1,2,3:T(8,128)(2,1)S(1)} copy(bf16[256,4,16,1,16]{4,3,2,1,0:T(2,128)(2,1)} %get-tuple-element.55) | data formatting | bytes 1048576 | tf_op jit(solution)/shard_map/transpose | solution.py:101
  608.7 5.2 constant_dynamic-update-slice_fusion.5
  614.0 6.8 constant_dynamic-update-slice_fusion.3
  620.7 6.9 constant_dynamic-update-slice_fusion.1
  627.7 4.3 constant_dynamic-update-slice_fusion
  631.9 25.6 %add_convert_fusion = bf16[64,2,4,2,2048]{4,0,3,2,1:T(8,128)(2,1)} fusion(bf16[64,2,4,2,2048]{4,0,3,2,1:T(8,128)(2,1)} %collective-permute-done.2, bf16[64,2,4,2,2048]{4,0,3,2,1:T(8,128)(2,1)} %collective-permute-done.1, bf16[64,2,4,2,2048]{4,0,3,2,1:T(8,128)(2,1)} %collective-permute-done, bf16[64,2,7,2,2048]{4,0,3,2,1:T(8,128)(2,1)S(1)} %get-tuple-element.61, ...), kind=kLoop, calls=%fused_computation.11 | loop fusion | flops 100663296 | bytes 71434240 | tf_op jit(solution)/shard_map/convert_element_type | solution.py:68
  657.5 8.4 copy.93
  666.0 8.9 fusion.6
  674.9 4.3 multiply_convert_fusion.1
  679.2 7.2 pad_maximum_fusion
  686.4 16.1 %convert_bitcast_fusion = bf16[64,2,4,64,64]{3,4,2,1,0:T(8,128)(2,1)} fusion(bf16[64,2,4,64,64]{4,0,3,2,1:T(8,128)(2,1)} %bitcast.84, bf16[64,64,1,1,1]{1,0,2,3,4:T(8,128)(2,1)S(1)} %reshape.261), kind=kOutput, calls=%fused_computation.8 | convolution fusion | flops 270532608 | bytes 8396800 | tf_op jit(solution)/shard_map/dk,spfkb->spfdb/dot_general | solution.py:87
  702.5 12.3 %copy.98 = bf16[64,2,4,64,64]{4,0,3,2,1:T(8,128)(2,1)} copy(bf16[64,2,4,64,64]{3,4,2,1,0:T(8,128)(2,1)} %convert_bitcast_fusion) | data formatting | bytes 8388608 | tf_op jit(solution)/shard_map/convert_element_type | solution.py:90
  714.7 21.1 %copy.115 = bf16[4,32,64,2,2,64]{5,4,3,2,1,0:T(2,128)(2,1)} copy(bf16[4,32,64,2,2,64]{2,5,4,1,0,3:T(8,128)(2,1)} %bitcast.85) | data formatting | bytes 8388608 | tf_op jit(solution)/shard_map/while | solution.py:161
  735.9 17.5 %reshape.263 = bf16[4,2048,2,128]{3,2,1,0:T(2,128)(2,1)} reshape(bf16[4,32,64,2,2,64]{5,4,3,2,1,0:T(2,128)(2,1)} %copy.115) | data formatting | bytes 8388608 | tf_op jit(solution)/shard_map/while | solution.py:161
  753.3 270.3 %while.11 = (s32[]{:T(128)}, f32[4,1024,256]{2,0,1:T(4,128)}, bf16[4,2048,2,128]{3,2,1,0:T(2,128)(2,1)}, bf16[16,2,64,2,256]{4,3,2,1,0:T(2,128)(2,1)}, bf16[16,1...) while((s32[]{:T(128)}, f32[4,1024,256]{2,0,1:T(4,128)}, ...), condition=%wide.wide.region_3.4_spmd, body=%wide.wide.region_0.3_spmd.sunk | while | flops 541851648 | bytes 60817552 | solution.py:161
  755.1 4.8 convolution_convert_fusion.4
  759.9 7.1 convert_element_type.246
  767.1 19.7 %reduce-scatter.2.cloned.1.call-done = bf16[1024,1024]{1,0:T(8,128)(2,1)} async-done(((bf16[2048,1024]{1,0:T(8,128)(2,1)}), bf16[1024,1024]{1,0:T(8,128)(2,1)}) %reduce-scatter.2.cloned.1.call-update) | async-done | bytes 2097168 | tf_op jit(solution)/shard_map/while/body/eval_jaxpr/reduce_scatter | solution.py:153
  786.8 4.2 convert_multiply_fusion.3
  791.0 5.6 mul.771
  796.6 4.7 reduce_sum.11
  802.4 23.2 %dynamic_update_slice.6 = f32[4,1024,256]{2,0,1:T(4,128)} dynamic-update-slice(f32[4,1024,256]{2,0,1:T(4,128)} %get-tuple-element.146, f32[1,1024,256]{2,0,1:T(1,128)S(1)} %copy.133, s32[]{:T(128)S(6)} %copy.141, s32[]{:T(128)} %constant.58.clone.1..sunk, s32[]{:T(128)} %constant.58.clone.1..sunk) | dynamic-update-slice | bytes 2097156 | tf_op jit(solution)/shard_map/while/body/jit(dynamic_update_index_in_dim)/dynamic_update_slice | solution.py:161
  827.4 4.8 convolution_convert_fusion.4
  832.1 7.1 convert_element_type.246
  839.3 13.5 %reduce-scatter.2.cloned.1.call-done = bf16[1024,1024]{1,0:T(8,128)(2,1)} async-done(((bf16[2048,1024]{1,0:T(8,128)(2,1)}), bf16[1024,1024]{1,0:T(8,128)(2,1)}) %reduce-scatter.2.cloned.1.call-update) | async-done | bytes 2097168 | tf_op jit(solution)/shard_map/while/body/eval_jaxpr/reduce_scatter | solution.py:153
  857.0 5.6 mul.771
  862.6 4.7 reduce_sum.11
  868.4 23.2 %dynamic_update_slice.6 = f32[4,1024,256]{2,0,1:T(4,128)} dynamic-update-slice(f32[4,1024,256]{2,0,1:T(4,128)} %get-tuple-element.146, f32[1,1024,256]{2,0,1:T(1,128)S(1)} %copy.133, s32[]{:T(128)S(6)} %copy.141, s32[]{:T(128)} %constant.58.clone.1..sunk, s32[]{:T(128)} %constant.58.clone.1..sunk) | dynamic-update-slice | bytes 2097156 | tf_op jit(solution)/shard_map/while/body/jit(dynamic_update_index_in_dim)/dynamic_update_slice | solution.py:161
  893.4 4.8 convolution_convert_fusion.4
  898.2 7.1 convert_element_type.246
  905.3 13.5 %reduce-scatter.2.cloned.1.call-done = bf16[1024,1024]{1,0:T(8,128)(2,1)} async-done(((bf16[2048,1024]{1,0:T(8,128)(2,1)}), bf16[1024,1024]{1,0:T(8,128)(2,1)}) %reduce-scatter.2.cloned.1.call-update) | async-done | bytes 2097168 | tf_op jit(solution)/shard_map/while/body/eval_jaxpr/reduce_scatter | solution.py:153
  923.0 5.6 mul.771
  928.6 4.7 reduce_sum.11
  934.4 23.2 %dynamic_update_slice.6 = f32[4,1024,256]{2,0,1:T(4,128)} dynamic-update-slice(f32[4,1024,256]{2,0,1:T(4,128)} %get-tuple-element.146, f32[1,1024,256]{2,0,1:T(1,128)S(1)} %copy.133, s32[]{:T(128)S(6)} %copy.141, s32[]{:T(128)} %constant.58.clone.1..sunk, s32[]{:T(128)} %constant.58.clone.1..sunk) | dynamic-update-slice | bytes 2097156 | tf_op jit(solution)/shard_map/while/body/jit(dynamic_update_index_in_dim)/dynamic_update_slice | solution.py:161
  959.4 4.8 convolution_convert_fusion.4
  964.2 7.1 convert_element_type.246
  971.3 13.5 %reduce-scatter.2.cloned.1.call-done = bf16[1024,1024]{1,0:T(8,128)(2,1)} async-done(((bf16[2048,1024]{1,0:T(8,128)(2,1)}), bf16[1024,1024]{1,0:T(8,128)(2,1)}) %reduce-scatter.2.cloned.1.call-update) | async-done | bytes 2097168 | tf_op jit(solution)/shard_map/while/body/eval_jaxpr/reduce_scatter | solution.py:153
  984.8 4.2 convert_multiply_fusion.3
  989.0 5.6 mul.771
  994.7 4.7 reduce_sum.11
  1000.4 23.2 %dynamic_update_slice.6 = f32[4,1024,256]{2,0,1:T(4,128)} dynamic-update-slice(f32[4,1024,256]{2,0,1:T(4,128)} %get-tuple-element.146, f32[1,1024,256]{2,0,1:T(1,128)S(1)} %copy.133, s32[]{:T(128)S(6)} %copy.141, s32[]{:T(128)} %constant.58.clone.1..sunk, s32[]{:T(128)} %constant.58.clone.1..sunk) | dynamic-update-slice | bytes 2097156 | tf_op jit(solution)/shard_map/while/body/jit(dynamic_update_index_in_dim)/dynamic_update_slice | solution.py:161
  (64 shorter events, 43.3 us)
Async XLA Ops:
  6.5 24.4 %copy-start = (s32[256,8]{0,1:T(8,128)S(1)}, s32[256,8]{0,1:T(8,128)}, u32[]{:S(2)}) copy-start(s32[256,8]{0,1:T(8,128)} %param.10) | copy-start | bytes 24580
  6.5 24.7 %copy-start.5 = (bf16[16,512]{1,0:T(8,128)(2,1)S(1)}, bf16[16,512]{1,0:T(8,128)(2,1)}, u32[]{:S(2)}) copy-start(bf16[16,512]{1,0:T(8,128)(2,1)} %param.11) | copy-start | bytes 49156
  13.0 521.1 %copy-start.6 = (s32[256,8]{0,1:T(8,128)S(1)}, s32[256,8]{0,1:T(8,128)}, u32[]{:S(2)}) copy-start(s32[256,8]{0,1:T(8,128)} %param.9) | copy-start | bytes 24580
  13.0 595.7 %collective-permute-start.2 = (bf16[64,2,4,2,2048]{4,0,3,2,1:T(8,128)(2,1)}, bf16[64,2,4,2,2048]{4,0,3,2,1:T(8,128)(2,1)}, u32[]{:S(2)}, u32[]{:S(2)}) collective-permute-start(bf16[64,2,4,2,2048]{4,0,3,2,1:T(8,128)(2,1)} %copy.87), channel_id=1, source_target_pairs={{0,6},{2,8},{4,10},{6,12},{8,14},{1,7},{3,9},{5,11},{7,13},{9,15},... | collective-permute-start | bytes 12582920 | tf_op jit(solution)/shard_map/ppermute | solution.py:16
  17.3 596.6 %collective-permute-start.1 = (bf16[64,2,4,2,2048]{4,0,3,2,1:T(8,128)(2,1)}, bf16[64,2,4,2,2048]{4,0,3,2,1:T(8,128)(2,1)}, u32[]{:S(2)}, u32[]{:S(2)}) collective-permute-start(bf16[64,2,4,2,2048]{4,0,3,2,1:T(8,128)(2,1)} %copy.87), channel_id=1, source_target_pairs={{0,4},{2,6},{4,8},{6,10},{8,12},{10,14},{1,5},{3,7},{5,9},{7,11},{... | collective-permute-start | bytes 12582920 | tf_op jit(solution)/shard_map/ppermute | solution.py:16
  19.3 601.5 %collective-permute-start = (bf16[64,2,4,2,2048]{4,0,3,2,1:T(8,128)(2,1)}, bf16[64,2,4,2,2048]{4,0,3,2,1:T(8,128)(2,1)}, u32[]{:S(2)}, u32[]{:S(2)}) collective-permute-start(bf16[64,2,4,2,2048]{4,0,3,2,1:T(8,128)(2,1)} %copy.87), channel_id=1, source_target_pairs={{0,2},{2,4},{4,6},{6,8},{8,10},{10,12},{12,14},{1,3},{3,5},{5,7},{... | collective-permute-start | bytes 12582920 | tf_op jit(solution)/shard_map/ppermute | solution.py:16
  26.4 580.2 %collective-permute-start.3 = (bf16[64,2,3,2,2048]{4,0,3,2,1:T(8,128)(2,1)}, bf16[64,2,3,2,2048]{4,0,3,2,1:T(8,128)(2,1)}, u32[]{:S(2)}, u32[]{:S(2)}) collective-permute-start(bf16[64,2,3,2,2048]{4,0,3,2,1:T(8,128)(2,1)} %slice.153), channel_id=1, source_target_pairs={{0,8},{2,10},{4,12},{6,14},{1,9},{3,11},{5,13},{7,15},{16,24},{18,... | collective-permute-start | bytes 9437192 | tf_op jit(solution)/shard_map/ppermute | solution.py:16
  600.5 6.0 copy-start.4
  603.1 10.8 %copy-start.3 = (bf16[16,2,64,2,256]{4,3,2,1,0:T(2,128)(2,1)}, bf16[16,2,64,2,256]{4,3,2,1,0:T(2,128)(2,1)S(1)}, u32[]{:S(2)}) copy-start(bf16[16,2,64,2,256]{4,3,2,1,0:T(2,128)(2,1)S(1)} %copy.107) | copy-start | bytes 6291460
  620.7 6.9 copy-start.2
  753.3 33.5 %reduce-scatter.2.cloned.1.call-start = ((), (), s32[]{:S(2)}) async-start(), calls=%async_computation.1 | async-start | bytes 6291456 | tf_op jit(solution)/shard_map/while/body/eval_jaxpr/reduce_scatter | solution.py:153
  825.5 27.3 %reduce-scatter.2.cloned.1.call-start = ((), (), s32[]{:S(2)}) async-start(), calls=%async_computation.1 | async-start | bytes 6291456 | tf_op jit(solution)/shard_map/while/body/eval_jaxpr/reduce_scatter | solution.py:153
  891.6 27.3 %reduce-scatter.2.cloned.1.call-start = ((), (), s32[]{:S(2)}) async-start(), calls=%async_computation.1 | async-start | bytes 6291456 | tf_op jit(solution)/shard_map/while/body/eval_jaxpr/reduce_scatter | solution.py:153
  957.6 27.3 %reduce-scatter.2.cloned.1.call-start = ((), (), s32[]{:S(2)}) async-start(), calls=%async_computation.1 | async-start | bytes 6291456 | tf_op jit(solution)/shard_map/while/body/eval_jaxpr/reduce_scatter | solution.py:153
  1023.6 0.7 copy-start.1
Sparse Core Ops, SparseCore 0:
  767.2 19.5 reduce-scatter.1
  839.4 13.3 reduce-scatter.1
  905.5 13.3 reduce-scatter.1
  971.5 13.3 reduce-scatter.1
where the time goes:
time: 1040 us; the launch traced here: 1030 us
  blocking collectives  494 us (48%)
  local copies, waits for them, and re-layouts  322 us (31%)
  other arithmetic  83.4 us (8%)
  waiting for transfers between devices  60.2 us (6%)
  matrix products  44.7 us (4%)
  between operations  13.5 us (1%)
  starting transfers between devices  12.3 us (1%)
    all_gather x1, blocking collectives, body(): shard_rows = lax.all_gather(weight_blocks, 'tm', axis=0, tiled=True)  494 us
    dynamic_update_slice x8, local copies, waits for them, and re-layouts, body(): unused, detected = lax.scan(frame_power, jnp.zeros((), jnp.float32), turned)  97 us
    reduce_scatter x4, waiting for transfers between devices, frame_power(): lax.psum_scatter(partial_value.astype(jnp.bfloat16).astype(jnp.float32).a...  60.2 us
    while x3, local copies, waits for them, and re-layouts, body(): unused, detected = lax.scan(frame_power, jnp.zeros((), jnp.float32), turned)  40.8 us
    convert_element_type x4, local copies, waits for them, and re-layouts, frame_power(): partial_value.astype(jnp.bfloat16).astype(jnp.float32).astype(jnp.bfloat16)  28.6 us
    unnamed x19, local copies, waits for them, and re-layouts  28.2 us
    convert_element_type x1, other arithmetic, filter_frames(): return summed.astype(jnp.bfloat16)  25.6 us
    mul x4, local copies, waits for them, and re-layouts, detect(): return jnp.sum(shaped * shaped, axis=1)  22.6 us
  transfers between devices with their start and end apart: 8, of which 4 were waited for; matrix products, arithmetic and copies ran while one was open for 10% of the time, Pallas kernels for 0%

commit v1 on v0

v1 whole, which is shorter than its diff:
```python
import functools
import math

import jax
import jax.numpy as jnp
from jax import lax
from jax.experimental import pallas as pl
from jax.experimental.pallas import tpu as pltpu
from jax.sharding import PartitionSpec as P

SB = 16
G = 16
LANES = 128
MESH = pl.DeviceIdType.MESH


def share_stations_kernel(size, v_ref, w_ref, out_ref, rows_ref, hold, hold_w, local, send, recv, send_w, recv_w):
    me = lax.axis_index("tm")
    barrier = pltpu.get_barrier_semaphore()
    for step in range(1, size):
        pl.semaphore_signal(barrier, inc=1, device_id={"tm": lax.rem(me + step, size)}, device_id_type=MESH)
    pl.semaphore_wait(barrier, size - 1)
    copies = []
    for step in range(1, size):
        to = lax.rem(me + step, size)
        copies.append(pltpu.make_async_remote_copy(
            src_ref=w_ref, dst_ref=rows_ref.at[me], send_sem=send_w.at[step], recv_sem=recv_w.at[step],
            device_id={"tm": to}, device_id_type=MESH))
        copies.append(pltpu.make_async_remote_copy(
            src_ref=v_ref.at[to], dst_ref=out_ref.at[me], send_sem=send.at[step], recv_sem=recv.at[step],
            device_id={"tm": to}, device_id_type=MESH))
    for copy in copies:
        copy.start()
    for source, middle, target, index in ((v_ref.at[me], hold, out_ref.at[me], 0), (w_ref, hold_w, rows_ref.at[me], 1)):
        copy = pltpu.make_async_copy(source, middle, local.at[index])
        copy.start()
        copy.wait()
        copy = pltpu.make_async_copy(middle, target, local.at[index])
        copy.start()
        copy.wait()
    for copy in copies:
        copy.wait()


def share_stations(blocks, weight_rows):
    size = blocks.shape[0]
    return pl.pallas_call(
        functools.partial(share_stations_kernel, size),
        out_shape=(jax.ShapeDtypeStruct(blocks.shape, blocks.dtype),
                   jax.ShapeDtypeStruct((size,) + weight_rows.shape, weight_rows.dtype)),
        in_specs=[pl.BlockSpec(memory_space=pl.ANY)] * 2,
        out_specs=[pl.BlockSpec(memory_space=pl.ANY)] * 2,
        scratch_shapes=[
            pltpu.VMEM(blocks.shape[1:], blocks.dtype), pltpu.VMEM(weight_rows.shape, weight_rows.dtype),
            pltpu.SemaphoreType.DMA((2,)),
            pltpu.SemaphoreType.DMA((size,)), pltpu.SemaphoreType.DMA((size,)),
            pltpu.SemaphoreType.DMA((size,)), pltpu.SemaphoreType.DMA((size,)),
        ],
        compiler_params=pltpu.CompilerParams(collective_id=0, has_side_effects=True),
        name="share_stations",
    )(blocks, weight_rows)


def return_frames_kernel(size, z_ref, out_ref, hold, local, send, recv):
    me = lax.axis_index("tm")
    core = lax.axis_index("stn")
    others = [(step, side) for step in range(size) for side in range(2) if step or side]
    targets = [(lax.rem(me + step, size), lax.rem(core + side, 2)) for step, side in others]
    barrier = pltpu.get_barrier_semaphore()
    for to, to_core in targets:
        pl.semaphore_signal(barrier, inc=1, device_id={"tm": to, "stn": to_core}, device_id_type=MESH)
    pl.semaphore_wait(barrier, len(others))
    slot = core * size + me
    copies = []
    for index, (to, to_core) in enumerate(targets):
        copies.append(pltpu.make_async_remote_copy(
            src_ref=z_ref.at[to, to_core], dst_ref=out_ref.at[slot], send_sem=send.at[index], recv_sem=recv.at[index],
            device_id={"tm": to, "stn": to_core}, device_id_type=MESH))
    for copy in copies:
        copy.start()
    copy = pltpu.make_async_copy(z_ref.at[me, core], hold, local)
    copy.start()
    copy.wait()
    copy = pltpu.make_async_copy(hold, out_ref.at[slot], local)
    copy.start()
    copy.wait()
    for copy in copies:
        copy.wait()


def return_frames(blocks):
    size = blocks.shape[0]
    return pl.pallas_call(
        functools.partial(return_frames_kernel, size),
        out_shape=jax.ShapeDtypeStruct((2 * size,) + blocks.shape[2:], blocks.dtype),
        in_specs=[pl.BlockSpec(memory_space=pl.ANY)],
        out_specs=pl.BlockSpec(memory_space=pl.ANY),
        scratch_shapes=[
            pltpu.VMEM(blocks.shape[2:], blocks.dtype), pltpu.SemaphoreType.DMA,
            pltpu.SemaphoreType.DMA((2 * size - 1,)), pltpu.SemaphoreType.DMA((2 * size - 1,)),
        ],
        compiler_params=pltpu.CompilerParams(collective_id=1, has_side_effects=True),
        name="return_frames",
    )(blocks)


def transform_tables(first, stations):
    full = first * LANES
    a = jnp.arange(first, dtype=jnp.int32)
    l = jnp.arange(LANES, dtype=jnp.int32)
    angle = (a[:, None] * a[None, :] % first).astype(jnp.float32) * (2.0 * math.pi / first)
    cos, sin = jnp.cos(angle), jnp.sin(angle)
    one = jnp.stack([jnp.stack([cos, sin], axis=1), jnp.stack([-sin, cos], axis=1)], axis=0)
    eye = jnp.eye(stations, dtype=jnp.float32)
    one = one[:, :, None, None] * eye[None, None, :, :, None, None]
    one = one.reshape(2 * first * stations, stations * 2 * first)
    angle = (l[:, None] * l[None, :] % LANES).astype(jnp.float32) * (2.0 * math.pi / LANES)
    cos, sin = jnp.cos(angle), jnp.sin(angle)
    two = jnp.stack([jnp.stack([cos, -sin], axis=0), jnp.stack([sin, cos], axis=0)], axis=0)
    two = two.reshape(2, 2, LANES, 2, 8, 8).transpose(0, 2, 3, 4, 1, 5)
    two = two.reshape(2 * LANES, 2 * LANES)
    angle = (a[:, None] * l[None, :] % full).astype(jnp.float32) * (2.0 * math.pi / full)
    norm = 1.0 / math.sqrt(full)
    twist_cos = jnp.repeat(jnp.cos(angle) * norm, stations, axis=0)
    twist_sin = jnp.repeat(jnp.sin(angle) * norm, stations, axis=0)
    return one.astype(jnp.bfloat16), two.astype(jnp.bfloat16), twist_cos, twist_sin


def channelize_kernel(x_ref, taps_ref, one_ref, two_ref, cos_ref, sin_ref, z_ref, window, held):
    size, stations, _, frames, _, first, _ = x_ref.shape
    taps = taps_ref.shape[0]
    block = pl.program_id(1)

    @pl.when(block == 0)
    def _():
        window[0:taps] = jnp.zeros((taps,) + window.shape[1:], window.dtype)

        def fill(t, carry):
            for f in range(frames):
                window[taps + t * frames + f] = x_ref[t, :, 0, f]
            return carry
        lax.fori_loop(0, size, fill, 0)

    base = block * frames + 1

    def filter_rows(index, carry):
        s = index // 2
        r = lax.rem(index, 2)
        sums = [None] * frames
        for m in range(frames + taps - 1):
            x = window[base + m, s, r].astype(jnp.float32)
            for f in range(frames):
                k = f + taps - 1 - m
                if 0 <= k < taps:
                    term = taps_ref[k] * x
                    sums[f] = term if sums[f] is None else sums[f] + term
        for f in range(frames):
            held[f, pl.ds(pl.multiple_of(index * first, first), first)] = sums[f].astype(held.dtype)
        return carry
    lax.fori_loop(0, 2 * stations, filter_rows, 0)

    rows = first * stations
    for f in range(frames):
        y = jnp.dot(one_ref[...], held[f], preferred_element_type=jnp.float32)
        re, im = y[:rows], y[rows:]
        cos, sin = cos_ref[...], sin_ref[...]
        turned = jnp.concatenate([re * cos + im * sin, im * cos - re * sin], axis=1).astype(jnp.bfloat16)
        z = jnp.dot(turned, two_ref[...], preferred_element_type=jnp.float32).astype(z_ref.dtype)
        for h in range(2):
            z_ref[0, h, 0, f] = z[:, h * LANES:(h + 1) * LANES]


def channelize(x, taps, tables):
    size, stations, pols, frames, _, first, _ = x.shape
    one, two, cos, sin = tables
    rows = first * stations
    fixed = lambda a: pl.BlockSpec(a.shape, lambda p, j: (0,) * a.ndim)
    taps = taps.reshape(taps.shape[0], first, LANES)
    return pl.pallas_call(
        channelize_kernel,
        grid=(pols, size),
        out_shape=jax.ShapeDtypeStruct((size, 2, pols, frames, rows, LANES), jnp.bfloat16),
        in_specs=[
            pl.BlockSpec((size, stations, 1, frames, 2, first, LANES), lambda p, j: (0, 0, p, 0, 0, 0, 0)),
            fixed(taps), fixed(one), fixed(two), fixed(cos), fixed(sin),
        ],
        out_specs=pl.BlockSpec((1, 2, 1, frames, rows, LANES), lambda p, j: (j, 0, p, 0, 0, 0)),
        scratch_shapes=[
            pltpu.VMEM((size * frames + taps.shape[0], stations, 2, first, LANES), jnp.bfloat16),
            pltpu.VMEM((frames, 2 * rows, LANES), jnp.bfloat16),
        ],
        name="channelize",
    )(x, taps, one, two, cos, sin)


def beams_kernel(s_ref, w_ref, out_ref, turned):
    sources, pols, _, first, stations, _ = s_ref.shape
    groups, depth, wide = w_ref.shape
    beams = wide // 2
    for p in range(pols):
        def turn(c1, carry):
            tile = s_ref[:, p, 0, c1].reshape(depth, LANES)
            tile = tile.astype(jnp.float32).T.astype(jnp.bfloat16)
            for g in range(groups):
                turned[p, g, c1] = tile[g * 16:(g + 1) * 16]
            return carry
        lax.fori_loop(0, first, turn, 0)

    def group(g, carry):
        power = None
        for p in range(pols):
            rows = turned[p, g].reshape(first * 16, depth)
            y = jnp.dot(rows, w_ref[g], preferred_element_type=jnp.float32).reshape(first, 2, 8, wide)
            re = y[:, 0, :, :beams] - y[:, 1, :, beams:]
            im = y[:, 0, :, beams:] + y[:, 1, :, :beams]
            term = re * re + im * im
            power = term if power is None else power + term
        out_ref[0, g] = power
        return carry
    lax.fori_loop(0, groups, group, 0)


def form_beams(spectra, weights):
    sources, pols, frames, first, stations, _ = spectra.shape
    groups, depth, wide = weights.shape
    return pl.pallas_call(
        beams_kernel,
        grid=(frames,),
        out_shape=jax.ShapeDtypeStruct((frames, groups, first, 8, wide // 2), jnp.float32),
        in_specs=[
            pl.BlockSpec((sources, pols, 1, first, stations, LANES), lambda f: (0, 0, f, 0, 0, 0)),
            pl.BlockSpec(weights.shape, lambda f: (0, 0, 0)),
        ],
        out_specs=pl.BlockSpec((1, groups, first, 8, wide // 2), lambda f: (f, 0, 0, 0, 0)),
        scratch_shapes=[pltpu.VMEM((pols, groups, first, 16, depth), jnp.bfloat16)],
        name="form_beams",
    )(spectra, weights)


def beam_weights(use_mask, block_index, rows, half, groups):
    beams, blocks = block_index.shape
    ids = jnp.arange(rows.shape[0], dtype=jnp.int32)
    index = block_index.T.reshape(-1)
    mask = use_mask.T.reshape(-1)
    onehot = jnp.where(index[:, None] == ids[None, :], mask[:, None], 0).astype(jnp.bfloat16)
    width = groups * 2 * SB
    mine = lax.dynamic_slice_in_dim(rows, half * width, width, 1)
    picked = lax.dot_general(mine, onehot, (((0,), (1,)), ((), ())), preferred_element_type=jnp.float32)
    picked = picked.astype(jnp.bfloat16).reshape(groups, 2, SB, blocks, beams)
    return picked.transpose(0, 3, 2, 1, 4).reshape(groups, blocks * SB, 2 * beams)


def body(voltages, filter_taps, use_mask, block_index, weight_blocks):
    stations, pols, frames, _, channels = voltages.shape
    size = lax.axis_size("tm")
    first = channels // LANES
    share = stations // size
    blocks = voltages.reshape(size, share, pols, frames, 2, first, LANES)
    x, rows = share_stations(blocks, weight_blocks)
    tables = transform_tables(first, share)
    z = channelize(x, filter_taps, tables)
    spectra = return_frames(z)
    spectra = spectra.reshape(2 * size, pols, frames, first, share, LANES)
    groups = G // 2
    weights = beam_weights(use_mask, block_index, rows.reshape(-1, rows.shape[-1]), lax.axis_index("stn"), groups)
    power = form_beams(spectra, weights)
    return power.transpose(1, 3, 2, 0, 4).reshape(channels // 2, frames, -1)


def solution(mesh):
    in_specs = (
        P(("parts", "stn"), None, "tm", None, None),
        P(),
        P("parts", None),
        P("parts", None),
        P("tm", None),
    )
    out_specs = P("stn", "tm", "parts")
    return jax.shard_map(body, mesh=mesh, in_specs=in_specs, out_specs=out_specs, check_vma=False)
```

time: 1040 us -> 280 us (0.27)
  blocking collectives: 494 us -> 0 us
  local copies, waits for them, and re-layouts: 322 us -> 25.3 us
  Pallas kernels: 0 us -> 251 us
  other arithmetic: 83.4 us -> 1.69 us
  waiting for transfers between devices: 60.2 us -> 0 us
  matrix products: 44.7 us -> 1.26 us
  between operations: 13.5 us -> 0.13 us
  starting transfers between devices: 12.3 us -> 0 us
    all_gather x1 -> x0, blocking collectives: 494 us -> none  [body(): shard_rows = lax.all_gather(weight_blocks, 'tm', axis=0, tiled=True)]
    pallas_call x0 -> x4, Pallas kernels: none -> 251 us  [the longest x1 98 us: share_stations(): pl.pallas_call(functools.partial(share_stations_kernel, size), out_shape=...]
    dynamic_update_slice x8 -> x0, local copies, waits for them, and re-layouts: 97 us -> none  [body(): unused, detected = lax.scan(frame_power, jnp.zeros((), jnp.float32), turned)]
    reduce_scatter x4 -> x0, waiting for transfers between devices: 60.2 us -> none  [frame_power(): lax.psum_scatter(partial_value.astype(jnp.bfloat16).astype(jnp.float32).a...]
    convert_element_type x8 -> x3, local copies, waits for them, and re-layouts: 50.3 us -> 2.54 us  [the longest x1 1.64 us: transform_tables(): one.astype(jnp.bfloat16)]
    dot_general x7 -> x1, matrix products: 44.7 us -> 1.26 us  [beam_weights(): lax.dot_general(mine, onehot, (((0,), (1,)), ((), ())), preferred_element...]
    while x3 -> x0, local copies, waits for them, and re-layouts: 40.8 us -> none  [body(): unused, detected = lax.scan(frame_power, jnp.zeros((), jnp.float32), turned)]
    transpose x2 -> x1, local copies, waits for them, and re-layouts: 35.3 us -> 3.92 us  [body(): return power.transpose(1, 3, 2, 0, 4).reshape(channels // 2, frames, -1)]
  transfers between devices with their start and end apart: 8 -> 0, of which waited for: 4 -> 0; matrix products, arithmetic and copies ran while one was open for 10% -> 0% of each run, Pallas kernels for 0% -> 0%
where the time goes in v1:
time: 280 us; the launch traced here: 279 us
  Pallas kernels  251 us (90%)
  local copies, waits for them, and re-layouts  25.3 us (9%)
    pallas_call x1, Pallas kernels, share_stations(): pl.pallas_call(functools.partial(share_stations_kernel, size), out_shape=...  98 us
    pallas_call x1, Pallas kernels, return_frames(): pl.pallas_call(functools.partial(return_frames_kernel, size), out_shape=j...  95.3 us
    pallas_call x1, Pallas kernels, channelize(): pl.pallas_call(channelize_kernel, grid=(pols, size), out_shape=jax.ShapeD...  32.6 us
    pallas_call x1, Pallas kernels, form_beams(): pl.pallas_call(beams_kernel, grid=(frames,), out_shape=jax.ShapeDtypeStru...  24.8 us
    reshape x1, local copies, waits for them, and re-layouts, body(): blocks = voltages.reshape(size, share, pols, frames, 2, first, LANES)  7.58 us

profile of v1, /device:TPU:13, one launch (start us, length us, event | category | flops | bytes accessed | tf_op | source)
XLA Modules:
  0.0 279.1 jit_solution(10409237163178899515)
XLA Ops:
  0.0 0.7 copy.20
  0.7 0.7 copy.19
  1.4 0.1 fusion.27
  1.5 0.1 cosine_multiply_fusion
  1.6 0.1 sine_multiply_fusion
  1.6 0.1 fusion.24
  1.7 0.3 negate_convert_fusion
  2.1 0.1 copy.12
  2.3 0.8 copy.13.two_ref
  3.0 0.6 broadcast_bitcast_fusion
  3.7 1.6 copy.17
  5.3 1.1 multiply_convert_fusion
  6.3 1.6 convert_element_type.83.one_ref
  8.0 7.6 %reshape.213.v_ref = bf16[8,8,2,4,2,16,128]{6,5,4,3,2,1,0:T(8,128)(2,1)} reshape(bf16[64,2,4,2,2048]{4,3,2,1,0:T(2,128)(2,1)} %param.5) | data formatting | bytes 8388608 | tf_op jit(solution)/shard_map/reshape | solution.py:258
  15.6 98.0 %share_stations.1 = (bf16[8,8,2,4,2,16,128]{6,5,4,3,2,1,0:T(8,128)(2,1)}, bf16[8,16,512]{2,1,0:T(8,128)(2,1)}) custom-call(bf16[8,8,2,4,2,16,128]{6,5,4,3,2,1,0:T(8,128)(2,1)} %reshape.213.v_ref, bf16[16,512]{1,0:T(8,128)(2,1)} %w_ref.1), custom_call_target="tpu_custom_call" | custom-call | tf_op jit(solution)/shard_map/share_stations/pallas_call | solution.py:47
  113.6 32.6 %channelize.1.z_ref = bf16[8,2,2,4,128,128]{5,4,3,2,1,0:T(8,128)(2,1)} custom-call(bf16[8,8,2,4,2,16,128]{6,5,4,3,2,1,0:T(8,128)(2,1)} %get-tuple-element.7.x_ref, f32[16,16,128]{2,1,0:T(8,128)} %bitcast.41, bf16[256,256]{1,0:T(8,128)(2,1)} %convert_element_type.83.one_ref, bf16[256,256]{1,0:T(8,128)(2,1)} %copy.13.two_ref, ...), custom_call_target="tpu_custom_call" | custom-call | tf_op jit(solution)/shard_map/channelize/pallas_call | solution.py:179
  146.2 0.0 copy-start
  146.2 95.3 %return_frames.1 = bf16[16,2,4,128,128]{4,3,2,1,0:T(8,128)(2,1)} custom-call(bf16[8,2,2,4,128,128]{5,4,3,2,1,0:T(8,128)(2,1)} %channelize.1.z_ref), custom_call_target="tpu_custom_call" | custom-call | tf_op jit(solution)/shard_map/return_frames/pallas_call | solution.py:93
  241.5 0.0 copy-done
  241.5 1.3 convolution_convert_fusion
  242.8 0.3 copy.21
  243.1 1.1 copy.24
  244.2 1.5 reshape.220.w_ref
  245.7 24.8 %form_beams.1 = f32[4,8,16,8,256]{4,3,2,1,0:T(8,128)} custom-call(bf16[16,2,4,16,8,128]{5,4,3,2,1,0:T(8,128)(2,1)} %bitcast.35, bf16[8,128,512]{2,1,0:T(8,128)(2,1)} %reshape.220.w_ref), custom_call_target="tpu_custom_call" | custom-call | tf_op jit(solution)/shard_map/form_beams/pallas_call | solution.py:226
  270.5 3.9 %copy.15 = f32[8,8,16,4,256]{4,2,1,0,3:T(8,128)S(1)} copy(f32[8,8,16,4,256]{4,1,2,0,3:T(8,128)} %bitcast.36) | data formatting | bytes 8388608 | tf_op jit(solution)/shard_map/transpose | solution.py:267
  274.4 4.7 %copy.16 = f32[1024,4,256]{2,1,0:T(4,128)} copy(f32[1024,4,256]{2,0,1:T(8,128)S(1)} %bitcast.37) | data formatting | bytes 8388608 | tf_op jit(solution)/shard_map/reshape | solution.py:267
  (7 shorter events, 0.1 us)
Async XLA Ops:
  146.2 95.3 %copy-start = (bf16[8,16,512]{2,1,0:T(8,128)(2,1)S(1)}, bf16[8,16,512]{2,1,0:T(8,128)(2,1)}, u32[]{:S(2)}) copy-start(bf16[8,16,512]{2,1,0:T(8,128)(2,1)} %get-tuple-element.8) | copy-start | bytes 393220

commit v2 on v0

v2 whole, which is shorter than its diff:
```python
import functools
import math

import jax
import jax.numpy as jnp
from jax import lax
from jax.experimental import pallas as pl
from jax.experimental.pallas import tpu as pltpu
from jax.sharding import PartitionSpec as P

SB = 16
G = 16
LANES = 128
MESH = pl.DeviceIdType.MESH


def transform_tables(first, stations):
    full = first * LANES
    a = jnp.arange(first, dtype=jnp.int32)
    l = jnp.arange(LANES, dtype=jnp.int32)
    angle = (a[:, None] * a[None, :] % first).astype(jnp.float32) * (2.0 * math.pi / first)
    cos, sin = jnp.cos(angle), jnp.sin(angle)
    one = jnp.stack([jnp.stack([cos, sin], axis=1), jnp.stack([-sin, cos], axis=1)], axis=0)
    eye = jnp.eye(stations, dtype=jnp.float32)
    one = one[:, :, None, None] * eye[None, None, :, :, None, None]
    one = one.reshape(2 * first * stations, stations * 2 * first)
    angle = (l[:, None] * l[None, :] % LANES).astype(jnp.float32) * (2.0 * math.pi / LANES)
    cos, sin = jnp.cos(angle), jnp.sin(angle)
    two = jnp.stack([jnp.stack([cos, -sin], axis=0), jnp.stack([sin, cos], axis=0)], axis=0)
    two = two.reshape(2, 2, LANES, 2, 8, 8).transpose(0, 2, 3, 4, 1, 5)
    two = two.reshape(2 * LANES, 2 * LANES)
    angle = (a[:, None] * l[None, :] % full).astype(jnp.float32) * (2.0 * math.pi / full)
    norm = 1.0 / math.sqrt(full)
    twist_cos = jnp.repeat(jnp.cos(angle) * norm, stations, axis=0)
    twist_sin = jnp.repeat(jnp.sin(angle) * norm, stations, axis=0)
    return one.astype(jnp.bfloat16), two.astype(jnp.bfloat16), twist_cos, twist_sin


def kernel(size, v_ref, rows_ref, onehot_ref, taps_ref, one_ref, two_ref, cos_ref, sin_ref, out_ref,
           x, window, held, z, r, table, weights, turned,
           local, send_w, recv_w, send_x, recv_x, send_z, recv_z):
    me = lax.axis_index("tm")
    core = lax.axis_index("stn")
    pols, _, stations, frames, _, first, _ = x.shape
    taps = taps_ref.shape[0]
    rows = first * stations
    groups, depth, wide = weights.shape
    beams = wide // 2
    slot = core * size + me

    barrier = pltpu.get_barrier_semaphore()
    for step in range(size):
        for side in range(2):
            if step or side:
                pl.semaphore_signal(
                    barrier, inc=1, device_id={"tm": lax.rem(me + step, size), "stn": lax.rem(core + side, 2)},
                    device_id_type=MESH)
    pl.semaphore_wait(barrier, 2 * size - 1)

    def weight_copy(step):
        return pltpu.make_async_remote_copy(
            src_ref=rows_ref, dst_ref=table.at[me], send_sem=send_w.at[step], recv_sem=recv_w.at[step],
            device_id={"tm": lax.rem(me + step, size)}, device_id_type=MESH)

    def voltage_copy(p, step):
        to = lax.rem(me + step, size)
        return pltpu.make_async_remote_copy(
            src_ref=v_ref.at[to, :, p], dst_ref=x.at[p, me], send_sem=send_x.at[p, step], recv_sem=recv_x.at[p, step],
            device_id={"tm": to}, device_id_type=MESH)

    def spectra_copy(p, step, side):
        to = lax.rem(me + step, size)
        to_core = lax.rem(core + side, 2)
        return pltpu.make_async_remote_copy(
            src_ref=z.at[p, to, to_core], dst_ref=r.at[p, slot],
            send_sem=send_z.at[p, step, side], recv_sem=recv_z.at[p, step, side],
            device_id={"tm": to, "stn": to_core}, device_id_type=MESH)

    for step in range(1, size):
        weight_copy(step).start()
    for p in range(pols):
        for step in range(1, size):
            voltage_copy(p, step).start()
    own = [pltpu.make_async_copy(v_ref.at[me, :, p], x.at[p, me], local.at[p]) for p in range(pols)]
    own.append(pltpu.make_async_copy(rows_ref, table.at[me], local.at[pols]))
    for copy in own:
        copy.start()

    window[0:taps] = jnp.zeros((taps,) + window.shape[1:], window.dtype)
    for step in range(1, size):
        weight_copy(step).wait()
    own[pols].wait()
    width = groups * 2 * SB
    mine = table[:, :, pl.ds(pl.multiple_of(core * width, width), width)].reshape(-1, width)
    mine = mine.astype(jnp.float32).T.astype(jnp.bfloat16)

    def pick(q, carry):
        picked = jnp.dot(mine, onehot_ref[q], preferred_element_type=jnp.float32).astype(jnp.bfloat16)
        for g in range(groups):
            for part in range(2):
                low = (2 * g + part) * SB
                weights[g, pl.ds(pl.multiple_of(q * SB, SB), SB), part * beams:(part + 1) * beams] = picked[low:low + SB]
        return carry
    lax.fori_loop(0, depth // SB, pick, 0)

    for p in range(pols):
        for step in range(1, size):
            voltage_copy(p, step).wait_recv()
        own[p].wait()

        def fill(t, carry):
            for f in range(frames):
                window[taps + t * frames + f] = x[p, t, :, f]
            return carry
        lax.fori_loop(0, size, fill, 0)

        def block(step, carry):
            to = lax.rem(me + step, size)
            base = to * frames + 1

            def filter_rows(index, carry):
                s = index // 2
                part = lax.rem(index, 2)
                sums = [None] * frames
                for m in range(frames + taps - 1):
                    sample = window[base + m, s, part].astype(jnp.float32)
                    for f in range(frames):
                        k = f + taps - 1 - m
                        if 0 <= k < taps:
                            term = taps_ref[k] * sample
                            sums[f] = term if sums[f] is None else sums[f] + term
                for f in range(frames):
                    held[f, pl.ds(pl.multiple_of(index * first, first), first)] = sums[f].astype(held.dtype)
                return carry
            lax.fori_loop(0, 2 * stations, filter_rows, 0)

            def transform(f, carry):
                y = jnp.dot(one_ref[...], held[f], preferred_element_type=jnp.float32)
                re, im = y[:rows], y[rows:]
                cos, sin = cos_ref[...], sin_ref[...]
                twisted = jnp.concatenate([re * cos + im * sin, im * cos - re * sin], axis=1).astype(jnp.bfloat16)
                spectra = jnp.dot(twisted, two_ref[...], preferred_element_type=jnp.float32)
                for h in range(2):
                    z[p, to, h, f] = spectra[:, h * LANES:(h + 1) * LANES].reshape(first, stations, LANES).astype(z.dtype)
                return carry
            lax.fori_loop(0, frames, transform, 0)

            @pl.when(step < size)
            def _():
                spectra_copy(p, lax.rem(step, size), 0).start()
            spectra_copy(p, lax.rem(step, size), 1).start()
            return carry
        lax.fori_loop(1, size + 1, block, 0)
        copy = pltpu.make_async_copy(z.at[p, me, core], r.at[p, slot], local.at[p])
        copy.start()
        copy.wait()

    for p in range(pols):
        for step in range(size):
            for side in range(2):
                if step or side:
                    spectra_copy(p, step, side).wait_recv()

        def frame(f, carry):
            def turn(c1, carry):
                tile = r[p, :, f, c1].reshape(depth, LANES)
                tile = tile.astype(jnp.float32).T.astype(jnp.bfloat16)
                for g in range(groups):
                    turned[g, c1] = tile[g * 16:(g + 1) * 16]
                return carry
            lax.fori_loop(0, first, turn, 0)

            def group(g, carry):
                y = jnp.dot(turned[g].reshape(first * 16, depth), weights[g], preferred_element_type=jnp.float32)
                y = y.reshape(first, 2, 8, wide)
                re = y[:, 0, :, :beams] - y[:, 1, :, beams:]
                im = y[:, 0, :, beams:] + y[:, 1, :, :beams]
                term = re * re + im * im
                out_ref[f, g] = term if p == 0 else out_ref[f, g] + term
                return carry
            lax.fori_loop(0, groups, group, 0)
            return carry
        lax.fori_loop(0, frames, frame, 0)

    for p in range(pols):
        for step in range(size):
            if step:
                voltage_copy(p, step).wait_send()
            for side in range(2):
                if step or side:
                    spectra_copy(p, step, side).wait_send()


def fused(v, weight_rows, onehot, taps, tables):
    size, stations, pols, frames, _, first, _ = v.shape
    groups = G // 2
    blocks, _, beams = onehot.shape
    depth = blocks * SB
    rows = first * stations
    taps = taps.reshape(taps.shape[0], first, LANES)
    bf16 = jnp.bfloat16
    dma = pltpu.SemaphoreType.DMA
    vmem = pl.BlockSpec(memory_space=pltpu.VMEM)
    hbm = pl.BlockSpec(memory_space=pl.ANY)
    return pl.pallas_call(
        functools.partial(kernel, size),
        out_shape=jax.ShapeDtypeStruct((frames, groups, first, 8, beams), jnp.float32),
        in_specs=[hbm, vmem] + [vmem] * 6,
        out_specs=vmem,
        scratch_shapes=[
            pltpu.VMEM((pols, size, stations, frames, 2, first, LANES), bf16),
            pltpu.VMEM((size * frames + taps.shape[0], stations, 2, first, LANES), bf16),
            pltpu.VMEM((frames, 2 * rows, LANES), bf16),
            pltpu.VMEM((pols, size, 2, frames, first, stations, LANES), bf16),
            pltpu.VMEM((pols, 2 * size, frames, first, stations, LANES), bf16),
            pltpu.VMEM((size,) + weight_rows.shape, bf16),
            pltpu.VMEM((groups, depth, 2 * beams), bf16),
            pltpu.VMEM((groups, first, 16, depth), bf16),
            dma((pols + 1,)), dma((size,)), dma((size,)),
            dma((pols, size)), dma((pols, size)), dma((pols, size, 2)), dma((pols, size, 2)),
        ],
        compiler_params=pltpu.CompilerParams(collective_id=0, has_side_effects=True, vmem_limit_bytes=60 << 20),
        name="fused_beams",
    )(v, weight_rows, onehot, taps, *tables)


def body(voltages, filter_taps, use_mask, block_index, weight_blocks):
    stations, pols, frames, _, channels = voltages.shape
    size = lax.axis_size("tm")
    first = channels // LANES
    share = stations // size
    blocks = voltages.reshape(size, share, pols, frames, 2, first, LANES)
    ids = jnp.arange(size * weight_blocks.shape[0], dtype=jnp.int32)
    onehot = jnp.where(
        block_index.T[:, None, :] == ids[None, :, None], use_mask.T[:, None, :], 0).astype(jnp.bfloat16)
    power = fused(blocks, weight_blocks, onehot, filter_taps, transform_tables(first, share))
    return power.transpose(1, 3, 2, 0, 4).reshape(channels // 2, frames, -1)


def solution(mesh):
    in_specs = (
        P(("parts", "stn"), None, "tm", None, None),
        P(),
        P("parts", None),
        P("parts", None),
        P("tm", None),
    )
    out_specs = P("stn", "tm", "parts")
    return jax.shard_map(body, mesh=mesh, in_specs=in_specs, out_specs=out_specs, check_vma=False)
```

time: 1040 us -> 233 us (0.22)
  blocking collectives: 494 us -> 0 us
  local copies, waits for them, and re-layouts: 322 us -> 21 us
  Pallas kernels: 0 us -> 208 us
  other arithmetic: 83.4 us -> 3.38 us
  waiting for transfers between devices: 60.2 us -> 0 us
  matrix products: 44.7 us -> 0 us
  between operations: 13.5 us -> 0.09 us
  starting transfers between devices: 12.3 us -> 0 us
    all_gather x1 -> x0, blocking collectives: 494 us -> none  [body(): shard_rows = lax.all_gather(weight_blocks, 'tm', axis=0, tiled=True)]
    pallas_call x0 -> x1, Pallas kernels: none -> 208 us  [fused(): pl.pallas_call(functools.partial(kernel, size), out_shape=jax.ShapeDtypeS...]
    dynamic_update_slice x8 -> x0, local copies, waits for them, and re-layouts: 97 us -> none  [body(): unused, detected = lax.scan(frame_power, jnp.zeros((), jnp.float32), turned)]
    reduce_scatter x4 -> x0, waiting for transfers between devices: 60.2 us -> none  [frame_power(): lax.psum_scatter(partial_value.astype(jnp.bfloat16).astype(jnp.float32).a...]
    convert_element_type x8 -> x3, local copies, waits for them, and re-layouts: 50.3 us -> 2.54 us  [the longest x1 1.64 us: transform_tables(): one.astype(jnp.bfloat16)]
    dot_general x7 -> x0, matrix products: 44.7 us -> none  [the longest x4 19.2 us: form_beams(): jnp.einsum('gmk,gkn->gmn', reshaped, matrices, preferred_element_type=jnp...]
    while x3 -> x0, local copies, waits for them, and re-layouts: 40.8 us -> none  [body(): unused, detected = lax.scan(frame_power, jnp.zeros((), jnp.float32), turned)]
    transpose x2 -> x1, local copies, waits for them, and re-layouts: 35.3 us -> 3.92 us  [body(): return power.transpose(1, 3, 2, 0, 4).reshape(channels // 2, frames, -1)]
  transfers between devices with their start and end apart: 8 -> 0, of which waited for: 4 -> 0; matrix products, arithmetic and copies ran while one was open for 10% -> 0% of each run, Pallas kernels for 0% -> 0%
where the time goes in v2:
time: 233 us
  Pallas kernels  208 us (89%)
  local copies, waits for them, and re-layouts  21 us (9%)
  other arithmetic  3.38 us (1%)
    pallas_call x1, Pallas kernels, fused(): pl.pallas_call(functools.partial(kernel, size), out_shape=jax.ShapeDtypeS...  208 us
    reshape x1, local copies, waits for them, and re-layouts, body(): blocks = voltages.reshape(size, share, pols, frames, 2, first, LANES)  7.58 us
    reshape x1, local copies, waits for them, and re-layouts, body(): return power.transpose(1, 3, 2, 0, 4).reshape(channels // 2, frames, -1)  4.71 us

profile of v2, /device:TPU:13, one launch (start us, length us, event | category | flops | bytes accessed | tf_op | source)
XLA Modules:
  0.0 232.6 jit_solution(7804371708640148476)
XLA Ops:
  0.0 0.1 fusion.23
  0.1 0.1 cosine_multiply_fusion
  0.1 0.1 sine_multiply_fusion
  0.2 0.1 fusion.20
  0.3 0.3 negate_convert_fusion
  0.7 0.1 copy.10
  0.9 0.8 copy.11.two_ref
  1.6 0.7 broadcast_bitcast_fusion
  2.3 1.6 copy.14
  3.9 1.7 select_convert_fusion.onehot_ref
  5.6 1.1 multiply_convert_fusion
  6.6 1.6 convert_element_type.81.one_ref
  8.3 7.6 %reshape.201.v_ref = bf16[8,8,2,4,2,16,128]{6,5,4,3,2,1,0:T(8,128)(2,1)} reshape(bf16[64,2,4,2,2048]{4,3,2,1,0:T(2,128)(2,1)} %param.5) | data formatting | bytes 8388608 | tf_op jit(solution)/shard_map/reshape | solution.py:232
  15.9 208.1 %fused_beams.1 = f32[4,8,16,8,256]{4,3,2,1,0:T(8,128)} custom-call(bf16[8,8,2,4,2,16,128]{6,5,4,3,2,1,0:T(8,128)(2,1)} %reshape.201.v_ref, bf16[16,512]{1,0:T(8,128)(2,1)} %rows_ref.1, bf16[8,128,256]{2,1,0:T(8,128)(2,1)} %select_convert_fusion.onehot_ref, f32[16,16,128]{2,1,0:T(8,128)} %bitcast.25, bf16[256,256]{1,0:T(8,128)(2,1)} %convert_element_type.81.one_ref, ...), custom_call_target="tpu_custom_call" | custom-call | tf_op jit(solution)/shard_map/fused_beams/pallas_call | solution.py:205
  224.0 3.9 %copy.12 = f32[8,8,16,4,256]{4,2,1,0,3:T(8,128)S(1)} copy(f32[8,8,16,4,256]{4,1,2,0,3:T(8,128)} %bitcast.23) | data formatting | bytes 8388608 | tf_op jit(solution)/shard_map/transpose | solution.py:237
  227.9 4.7 %copy.13 = f32[1024,4,256]{2,1,0:T(4,128)} copy(f32[1024,4,256]{2,0,1:T(8,128)S(1)} %bitcast.24) | data formatting | bytes 8388608 | tf_op jit(solution)/shard_map/reshape | solution.py:237
  (7 shorter events, 0.1 us)

commit v3 on v2

v3 whole, which is shorter than its diff:
```python
import functools
import math

import jax
import jax.numpy as jnp
import numpy as np
from jax import lax
from jax.experimental import pallas as pl
from jax.experimental.pallas import tpu as pltpu
from jax.sharding import PartitionSpec as P

SB = 16
G = 16
LANES = 128
MESH = pl.DeviceIdType.MESH


def transform_tables(first, stations):
    full = first * LANES
    a = np.arange(first)
    l = np.arange(LANES)

    def waves(product, period):
        angle = (product % period).astype(np.float32) * np.float32(2.0 * math.pi / period)
        return np.cos(angle), np.sin(angle)

    cos, sin = waves(a[:, None] * a[None, :], first)
    one = np.stack([np.stack([cos, sin], axis=-1), np.stack([-sin, cos], axis=-1)], axis=0)
    eye = np.eye(stations, dtype=np.float32)
    one = one[:, :, None, None] * eye[None, None, :, :, None, None]
    one = one.reshape(2 * first * stations, stations * 2 * first)
    cos, sin = waves(l[:, None] * l[None, :], LANES)
    two = np.stack([np.stack([cos, -sin], axis=0), np.stack([sin, cos], axis=0)], axis=0)
    two = two.reshape(2, 2, LANES, 2, 8, 8).transpose(0, 2, 3, 4, 1, 5)
    two = two.reshape(2 * LANES, 2 * LANES)
    cos, sin = waves(a[:, None] * l[None, :], full)
    norm = np.float32(1.0 / math.sqrt(full))
    cos = np.repeat(cos * norm, stations, axis=0)
    sin = np.repeat(sin * norm, stations, axis=0)
    return jnp.asarray(one, jnp.bfloat16), jnp.asarray(two, jnp.bfloat16), jnp.asarray(cos), jnp.asarray(sin)


def kernel(size, v_ref, rows_ref, onehot_ref, taps_ref, one_ref, two_ref, cos_ref, sin_ref, out_ref,
           x, window, held, z, r, table, weights, turned, total,
           local, send_w, recv_w, send_x, recv_x, send_z, recv_z):
    me = lax.axis_index("tm")
    core = lax.axis_index("stn")
    pols, _, stations, frames, first, _ = x.shape
    first //= 2
    half = frames // 2
    taps = taps_ref.shape[0]
    rows = first * stations
    groups, depth, wide = weights.shape
    beams = wide // 2
    slot = core * size + me

    barrier = pltpu.get_barrier_semaphore()
    for step in range(size):
        for side in range(2):
            if step or side:
                pl.semaphore_signal(
                    barrier, inc=1, device_id={"tm": lax.rem(me + step, size), "stn": lax.rem(core + side, 2)},
                    device_id_type=MESH)
    pl.semaphore_wait(barrier, 2 * size - 1)

    def weight_copy(step):
        return pltpu.make_async_remote_copy(
            src_ref=rows_ref, dst_ref=table.at[me], send_sem=send_w.at[step], recv_sem=recv_w.at[step],
            device_id={"tm": lax.rem(me + step, size)}, device_id_type=MESH)

    def voltage_copy(p, step):
        to = lax.rem(me + step, size)
        return pltpu.make_async_remote_copy(
            src_ref=v_ref.at[to, :, p], dst_ref=x.at[p, me], send_sem=send_x.at[p, step], recv_sem=recv_x.at[p, step],
            device_id={"tm": to}, device_id_type=MESH)

    def spectra_copy(p, step, side, late):
        to = lax.rem(me + step, size)
        to_core = lax.rem(core + side, 2)
        return pltpu.make_async_remote_copy(
            src_ref=z.at[p, to, to_core, pl.ds(late * half, half)], dst_ref=r.at[p, slot, pl.ds(late * half, half)],
            send_sem=send_z.at[p, step, side, late], recv_sem=recv_z.at[p, step, side, late],
            device_id={"tm": to, "stn": to_core}, device_id_type=MESH)

    def send_spectra(p, step, late):
        @pl.when(step < size)
        def _():
            spectra_copy(p, lax.rem(step, size), 0, late).start()
        spectra_copy(p, lax.rem(step, size), 1, late).start()

    for step in range(1, size):
        weight_copy(step).start()
    for p in range(pols):
        for step in range(1, size):
            voltage_copy(p, step).start()
    own = [pltpu.make_async_copy(v_ref.at[me, :, p], x.at[p, me], local.at[p]) for p in range(pols)]
    own.append(pltpu.make_async_copy(rows_ref, table.at[me], local.at[pols]))
    for copy in own:
        copy.start()

    window[0:taps] = jnp.zeros((taps,) + window.shape[1:], window.dtype)
    for step in range(1, size):
        weight_copy(step).wait()
    own[pols].wait()
    width = groups * 2 * SB
    mine = table[:, :, pl.ds(pl.multiple_of(core * width, width), width)].reshape(-1, width)
    mine = mine.astype(jnp.float32).T.astype(jnp.bfloat16)

    def pick(q, carry):
        picked = jnp.dot(mine, onehot_ref[q], preferred_element_type=jnp.float32).astype(jnp.bfloat16)
        for g in range(groups):
            for part in range(2):
                low = (2 * g + part) * SB
                weights[g, pl.ds(pl.multiple_of(q * SB, SB), SB), part * beams:(part + 1) * beams] = picked[low:low + SB]
        return carry
    lax.fori_loop(0, depth // SB, pick, 0)

    for p in range(pols):
        for step in range(1, size):
            voltage_copy(p, step).wait_recv()
        own[p].wait()

        def fill(t, carry):
            for f in range(frames):
                window[taps + t * frames + f] = x[p, t, :, f]
            return carry
        lax.fori_loop(0, size, fill, 0)

        def block(step, carry):
            to = lax.rem(me + step, size)
            base = to * frames + 1

            def filter_rows(index, carry):
                s = index // 2
                part = lax.rem(index, 2)
                sums = [None] * frames
                for m in range(frames + taps - 1):
                    sample = window[base + m, s, pl.ds(pl.multiple_of(part * first, first), first)].astype(jnp.float32)
                    for f in range(frames):
                        k = f + taps - 1 - m
                        if 0 <= k < taps:
                            term = taps_ref[k, part] * sample
                            sums[f] = term if sums[f] is None else sums[f] + term
                for f in range(frames):
                    held[f, pl.ds(pl.multiple_of(index * first, first), first)] = sums[f].astype(held.dtype)
                return carry
            lax.fori_loop(0, 2 * stations, filter_rows, 0)

            def transform(f, carry):
                y = jnp.dot(one_ref[...], held[f], preferred_element_type=jnp.float32)
                re, im = y[:rows], y[rows:]
                cos, sin = cos_ref[...], sin_ref[...]
                twisted = jnp.concatenate([re * cos + im * sin, im * cos - re * sin], axis=1).astype(jnp.bfloat16)
                spectra = jnp.dot(twisted, two_ref[...], preferred_element_type=jnp.float32)
                for h in range(2):
                    z[p, to, h, f] = spectra[:, h * LANES:(h + 1) * LANES].reshape(first, stations, LANES).astype(z.dtype)
                return carry
            lax.fori_loop(0, frames, transform, 0)

            send_spectra(p, step, 0)
            if p < pols - 1:
                send_spectra(p, step, 1)
            return carry
        lax.fori_loop(1, size + 1, block, 0)
        if p == pols - 1:
            def rest(step, carry):
                send_spectra(p, step, 1)
                return carry
            lax.fori_loop(1, size + 1, rest, 0)
        copy = pltpu.make_async_copy(z.at[p, me, core], r.at[p, slot], local.at[p])
        copy.start()
        copy.wait()

    pieces = beams // LANES
    pitch = pieces * frames

    def frame_of(p, f):
        def turn(c1, carry):
            tile = r[p, :, f, c1].reshape(depth, LANES).T
            for g in range(groups):
                turned[g, c1] = tile[g * 16:(g + 1) * 16]
            return carry
        lax.fori_loop(0, first, turn, 0)

        def group(g, carry):
            y = jnp.dot(turned[g].reshape(first * 16, depth), weights[g], preferred_element_type=jnp.float32)
            y = y.reshape(first, 2, 8, wide)
            re = y[:, 0, :, :beams] - y[:, 1, :, beams:]
            im = y[:, 0, :, beams:] + y[:, 1, :, :beams]
            power = re * re + im * im
            if p > 0:
                power = total[f, g] + power
            if p < pols - 1:
                total[f, g] = power
            else:
                for c1 in range(first):
                    for piece in range(pieces):
                        row = g * (8 * first * pitch) + (c1 * pitch + piece * frames + f)
                        out_ref[pl.ds(row, 8, stride=first * pitch), :] = power[c1, :, piece * LANES:(piece + 1) * LANES]
            return carry
        lax.fori_loop(0, groups, group, 0)

    for p in range(pols):
        for late in range(2):
            for step in range(size):
                for side in range(2):
                    if step or side:
                        spectra_copy(p, step, side, late).wait_recv()

            def frame(f, carry):
                frame_of(p, f)
                return carry
            lax.fori_loop(late * half, (late + 1) * half, frame, 0)

    for p in range(pols):
        for step in range(size):
            if step:
                voltage_copy(p, step).wait_send()
            for side in range(2):
                if step or side:
                    for late in range(2):
                        spectra_copy(p, step, side, late).wait_send()


def fused(v, weight_rows, onehot, taps, tables):
    size, stations, pols, frames, first, _ = v.shape
    first //= 2
    groups = G // 2
    blocks, _, beams = onehot.shape
    depth = blocks * SB
    rows = first * stations
    taps = jnp.repeat(taps.reshape(taps.shape[0], first, LANES), 2, axis=1).reshape(-1, 2, first, LANES)
    bf16 = jnp.bfloat16
    dma = pltpu.SemaphoreType.DMA
    vmem = pl.BlockSpec(memory_space=pltpu.VMEM)
    hbm = pl.BlockSpec(memory_space=pl.ANY)
    return pl.pallas_call(
        functools.partial(kernel, size),
        out_shape=jax.ShapeDtypeStruct((groups * 8 * first * frames * beams // LANES, LANES), jnp.float32),
        in_specs=[hbm, vmem] + [vmem] * 6,
        out_specs=vmem,
        scratch_shapes=[
            pltpu.VMEM((pols, size, stations, frames, 2 * first, LANES), bf16),
            pltpu.VMEM((size * frames + taps.shape[0], stations, 2 * first, LANES), bf16),
            pltpu.VMEM((frames, 2 * rows, LANES), bf16),
            pltpu.VMEM((pols, size, 2, frames, first, stations, LANES), bf16),
            pltpu.VMEM((pols, 2 * size, frames, first, stations, LANES), bf16),
            pltpu.VMEM((size,) + weight_rows.shape, bf16),
            pltpu.VMEM((groups, depth, 2 * beams), bf16),
            pltpu.VMEM((groups, first, 16, depth), bf16),
            pltpu.VMEM((frames, groups, first, 8, beams), jnp.float32),
            dma((pols + 1,)), dma((size,)), dma((size,)),
            dma((pols, size)), dma((pols, size)), dma((pols, size, 2, 2)), dma((pols, size, 2, 2)),
        ],
        compiler_params=pltpu.CompilerParams(collective_id=0, has_side_effects=True, vmem_limit_bytes=60 << 20),
        name="fused_beams",
    )(v, weight_rows, onehot, taps, *tables)


def body(voltages, filter_taps, use_mask, block_index, weight_blocks):
    stations, pols, frames, _, channels = voltages.shape
    size = lax.axis_size("tm")
    first = channels // LANES
    share = stations // size
    blocks = voltages.reshape(size, share, pols, frames, 2, first, LANES).swapaxes(-3, -2)
    blocks = blocks.reshape(size, share, pols, frames, 2 * first, LANES)
    ids = jnp.arange(size * weight_blocks.shape[0], dtype=jnp.int32)
    onehot = jnp.where(
        block_index.T[:, None, :] == ids[None, :, None], use_mask.T[:, None, :], 0).astype(jnp.bfloat16)
    beams = block_index.shape[0]
    power = fused(blocks, weight_blocks, onehot, filter_taps, transform_tables(first, share))
    power = power.reshape(channels // 2, beams // LANES, frames, LANES)
    return power.swapaxes(1, 2).reshape(channels // 2, frames, beams)


def solution(mesh):
    in_specs = (
        P(("parts", "stn"), None, "tm", None, None),
        P(),
        P("parts", None),
        P("parts", None),
        P("tm", None),
    )
    out_specs = P("stn", "tm", "parts")
    return jax.shard_map(body, mesh=mesh, in_specs=in_specs, out_specs=out_specs, check_vma=False)
```

time: 233 us -> 209 us (0.90)
  local copies, waits for them, and re-layouts: 21 us -> 6.67 us
  Pallas kernels: 208 us -> 200 us
    reshape x3 -> x0, local copies, waits for them, and re-layouts: 13 us -> none  [the longest x1 7.58 us: body(): blocks = voltages.reshape(size, share, pols, frames, 2, first, LANES)]
    pallas_call x1, Pallas kernels: 208 us -> 200 us  [fused(): pl.pallas_call(functools.partial(kernel, size), out_shape=jax.ShapeDtypeS...]
    unnamed x2, local copies, waits for them, and re-layouts: 1.59 us -> 5.85 us
    transpose x1 -> x0, local copies, waits for them, and re-layouts: 3.92 us -> none  [body(): return power.transpose(1, 3, 2, 0, 4).reshape(channels // 2, frames, -1)]
    convert_element_type x3 -> x0, local copies, waits for them, and re-layouts: 2.54 us -> none  [the longest x1 1.64 us: transform_tables(): one.astype(jnp.bfloat16)]
where the time goes in v3:
time: 209 us
  Pallas kernels  200 us (96%)
  local copies, waits for them, and re-layouts  6.67 us (3%)
    pallas_call x1, Pallas kernels, fused(): pl.pallas_call(functools.partial(kernel, size), out_shape=jax.ShapeDtypeS...  200 us
    unnamed x2, local copies, waits for them, and re-layouts  5.85 us

profile of v3, /device:TPU:13, one launch (start us, length us, event | category | flops | bytes accessed | tf_op | source)
XLA Modules:
  0.0 208.6 jit_solution(391144624077038186)
XLA Ops:
  0.0 0.9 copy.12
  0.9 0.8 broadcast_in_dim.20
  1.8 1.7 select_convert_fusion.onehot_ref
  3.4 200.3 %fused_beams.1 = f32[8192,128]{1,0:T(8,128)} custom-call(bf16[8,8,2,4,32,128]{5,4,3,2,1,0:T(8,128)(2,1)} %bitcast.16, bf16[16,512]{1,0:T(8,128)(2,1)} %rows_ref.1, bf16[8,128,256]{2,1,0:T(8,128)(2,1)} %select_convert_fusion.onehot_ref, f32[16,2,16,128]{3,2,1,0:T(8,128)} %bitcast.17, bf16[256,256]{1,0:T(8,128)(2,1)} %constant.10.clone.one_ref, ...), custom_call_target="tpu_custom_call" | custom-call | tf_op jit(solution)/shard_map/fused_beams/pallas_call | solution.py:237
  203.7 4.9 %copy.14 = f32[1024,4,256]{2,1,0:T(4,128)} copy(f32[1024,4,256]{2,1,0:T(4,128)} %bitcast.15) | data formatting | bytes 8388608
